TPU v7x, 32 devices: a whole 2x2x4 slice. The times are simulated.
32 devices in a mesh: leaf: 8 (over z, core), sub: 4 (over y, x).
Axes of the slice: x: 2, y: 2, z: 4, core: 2. Of those that a mesh axis runs over, the one named last changes fastest.
Arguments:
- leaf_maps: float32 [32, 256, 1024], P('leaf', 'sub'), may hold values from -8 to 28, as said below
- order_one: int32 [8, 4], replicated, may hold values from 0 to 3, each once within a row
- order_two: int32 [4, 6], replicated, may hold values from 0 to 5, each once within a row
- top_data: float32 [16, 256, 256], P('leaf', 'sub'), may hold values from -6 to 6
Outputs:
- top_map: float32 [16, 256, 2048], P('leaf', 'sub')
- leaf_data: float32 [32, 256, 256], P('leaf', 'sub')
Inputs may be any that keep to these rules, and one draw needn't show every extreme that they name: Each leaf's block of 1024 rows of leaf_maps, read as a 1024 by 1024 matrix, is symmetric and positive definite.
All inputs are finite; a program needn't handle non-finite values. Where the computation divides by a largest or mean magnitude, that divisor is 1e-20 or more.
Results may differ from a plain program's by a relative error of at most 0.0001.
Values sent between devices are 32-bit elements; how exact they have to be, the bound alone decides.
No kernel may reach another device: no remote copies, remote signals or barrier semaphores. Data moves between devices by JAX's collectives and lax.ppermute only.
A program may use at most 64 MiB of HBM per device.

v0:
```python
import jax
import jax.numpy as jnp
from jax import lax
from jax.sharding import PartitionSpec as P

W = 256
K = 256
NS_STEPS = 4


def swapped(value, axis, apart):
    mask = 2**apart
    pairs = [(source, source ^ mask) for source in range(lax.axis_size(axis))]
    return lax.ppermute(value, axis, pairs)


def exact_dot(left_matrix, right_matrix):
    return jnp.dot(
        left_matrix,
        right_matrix,
        precision=lax.Precision.HIGHEST,
        preferred_element_type=jnp.float32,
    )


def interface_inverse(block_rows):
    slot_count, width_local, block_size = block_rows.shape
    full_block = lax.all_gather(block_rows, "sub", axis=1, tiled=True).reshape(
        block_size, block_size
    )
    row_bound = jnp.max(jnp.sum(jnp.abs(full_block), axis=1))
    iterate = jnp.eye(block_size, dtype=jnp.float32) / row_bound
    for iteration in range(NS_STEPS):
        iterate = 2.0 * iterate - exact_dot(exact_dot(full_block, iterate), iterate)
    return iterate


def shards(leaf_maps, order_one, order_two, top_data):
    width_local = leaf_maps.shape[1]
    group_index = lax.axis_index("leaf")
    member_index = lax.axis_index("sub")
    parity = group_index % 2
    is_first = parity == 0
    own_order = order_one[group_index]
    permuted = jnp.take(leaf_maps, own_order, axis=0)
    permuted = jnp.take(permuted.reshape(4, width_local, 4, W), own_order, axis=2).reshape(
        4, width_local, 4 * W
    )
    near_rows = permuted[:3]
    inner_piece = permuted[3]
    other_piece = swapped(inner_piece, "leaf", 0)
    first_piece = jnp.where(is_first, inner_piece, other_piece)
    second_piece = jnp.where(is_first, other_piece, inner_piece)
    block_one = first_piece[:, 3 * W :] + second_piece[:, 3 * W :]
    inverse_one = interface_inverse(block_one[None])
    coupling_one = near_rows[:, :, 3 * W :].reshape(3 * width_local, W)
    scaled_one = exact_dot(coupling_one, inverse_one)
    pieces = (
        lax.all_gather(first_piece[:, : 3 * W], "sub", axis=0, tiled=True),
        lax.all_gather(second_piece[:, : 3 * W], "sub", axis=0, tiled=True),
    )
    piece_rows = pieces[0].shape[0]
    joined = jnp.concatenate([pieces[0], pieces[1]], axis=1)
    coeff_part = scaled_one
    running_sum = exact_dot(coeff_part, joined)
    own_part = jnp.where(is_first, pieces[0], pieces[1]).reshape(piece_rows, 3, W)
    own_part = lax.dynamic_slice_in_dim(own_part, member_index * width_local, width_local, 2)
    kept_columns = own_part.reshape(piece_rows, 3 * width_local)
    product_one = running_sum
    right_one = kept_columns
    own_outer = near_rows[:, :, : 3 * W].reshape(3 * width_local, 3 * W)
    zero_one = jnp.zeros_like(own_outer)
    diagonal_one = jnp.where(
        is_first,
        jnp.concatenate([own_outer, zero_one], axis=1),
        jnp.concatenate([zero_one, own_outer], axis=1),
    )
    merged_one = (diagonal_one - product_one).reshape(3, width_local, 6 * W)
    node_index = group_index // 2
    node_first = node_index % 2 == 0
    node_order = order_two[node_index]
    node_rows = jnp.take(merged_one.reshape(3, width_local, 6, W), node_order, axis=2).reshape(
        3, width_local, 6 * W
    )
    position_table = jnp.sum(
        jnp.arange(6)[:, None] * (node_order[:, None] == jnp.arange(6)[None, :]).astype(jnp.int32),
        axis=0,
    )
    my_positions = jnp.take(position_table, 3 * parity + jnp.arange(3))
    slot_edges = node_order[4:6]
    slot_held = (slot_edges // 3 == parity).astype(jnp.float32)
    slot_piece = jnp.take(node_rows, slot_edges % 3, axis=0) * slot_held[:, None, None]
    node_piece = slot_piece + swapped(slot_piece, "leaf", 0)
    cousin_piece = swapped(node_piece, "leaf", 1)
    first_node = jnp.where(node_first, node_piece, cousin_piece)
    second_node = jnp.where(node_first, cousin_piece, node_piece)
    block_two = first_node[:, :, 4 * W :] + second_node[:, :, 4 * W :]
    inverse_two = interface_inverse(block_two)
    coupling_two = node_rows[:, :, 4 * W :].reshape(3 * width_local, 2 * W)
    scaled_two = exact_dot(coupling_two, inverse_two).reshape(3 * width_local, 2, W)
    top_first = 2 * (group_index % 4)
    pieces = (
        lax.all_gather(first_node[:, :, : 4 * W], "sub", axis=1, tiled=True),
        lax.all_gather(second_node[:, :, : 4 * W], "sub", axis=1, tiled=True),
    )
    piece_rows = pieces[0].shape[1]
    joined = jnp.concatenate([pieces[0], pieces[1]], axis=2)
    coeff_part = scaled_two.reshape(3 * width_local, 2 * piece_rows)
    running_sum = exact_dot(coeff_part, joined.reshape(2 * piece_rows, 8 * W))
    own_part = lax.dynamic_slice_in_dim(joined.reshape(2, piece_rows, 8, W), top_first, 2, 2)
    own_part = lax.dynamic_slice_in_dim(own_part, member_index * width_local, width_local, 3)
    kept_columns = own_part
    node_outer = node_rows[:, :, : 4 * W].reshape(3 * width_local, 4 * W)
    zero_two = jnp.zeros_like(node_outer)
    diagonal_two = jnp.where(
        node_first,
        jnp.concatenate([node_outer, zero_two], axis=1),
        jnp.concatenate([zero_two, node_outer], axis=1),
    )
    top_rows = (diagonal_two - running_sum).reshape(3, width_local, 8 * W)
    node_offset = 4 * (node_index % 2)
    buffer = jnp.zeros((8, width_local, 8 * W), jnp.float32)
    for row_slot in range(3):
        target = node_offset + my_positions[row_slot]
        marker = ((jnp.arange(8) == target) & (my_positions[row_slot] < 4)).astype(jnp.float32)
        buffer = buffer + marker[:, None, None] * top_rows[row_slot][None]
    upper_half = node_index % 2
    outgoing = lax.dynamic_slice_in_dim(buffer, 4 * (1 - upper_half), 4, 0)
    retained = lax.dynamic_slice_in_dim(buffer, 4 * upper_half, 4, 0)
    retained = retained + swapped(outgoing, "leaf", 1)
    outgoing_near = lax.dynamic_slice_in_dim(retained, 2 * (1 - parity), 2, 0)
    own_part = lax.dynamic_slice_in_dim(retained, 2 * parity, 2, 0)
    top_map = own_part + swapped(outgoing_near, "leaf", 0)
    partial_two = exact_dot(
        kept_columns.reshape(2 * W, 2 * width_local), top_data.reshape(2 * width_local, K)
    )
    partial_two = lax.psum(partial_two, "sub")
    spread = lax.dynamic_update_slice_in_dim(
        jnp.zeros((8, width_local, K), jnp.float32), top_data, top_first, 0
    )
    for bit_index in range(2):
        other_sum, other_spread = swapped((partial_two, spread), "leaf", bit_index)
        partial_two = partial_two + other_sum
        spread = spread + other_spread
    inner_two = -exact_dot(inverse_two, partial_two)
    inner_local = lax.dynamic_slice_in_dim(
        inner_two.reshape(2, W, K), member_index * width_local, width_local, 1
    )
    candidates = jnp.concatenate(
        [lax.dynamic_slice_in_dim(spread, node_offset, 4, 0), inner_local], axis=0
    )
    node_data = jnp.take(candidates, my_positions, axis=0)
    partial_one = exact_dot(right_one, node_data.reshape(3 * width_local, K))
    partial_one = lax.psum(partial_one, "sub")
    partial_one = partial_one + swapped(partial_one, "leaf", 0)
    inner_one = -exact_dot(inverse_one, partial_one)
    inner_slice = lax.dynamic_slice_in_dim(inner_one, member_index * width_local, width_local, 0)
    permuted_data = jnp.concatenate([node_data, inner_slice[None]], axis=0)
    restore = (own_order[:, None] == jnp.arange(4)[None, :]).astype(jnp.float32)
    leaf_data = jnp.zeros((4, width_local, K), jnp.float32)
    for position in range(4):
        leaf_data = leaf_data + restore[position][:, None, None] * permuted_data[position][None]
    return (top_map, leaf_data)


def solution(mesh):
    in_specs = (P("leaf", "sub", None), P(), P(), P("leaf", "sub", None))
    out_specs = (P("leaf", "sub", None), P("leaf", "sub", None))
    return jax.shard_map(shards, mesh=mesh, in_specs=in_specs, out_specs=out_specs, check_vma=False)
```

profile of v0, /device:TPU:0, one launch (start us, length us, event | category | flops | bytes accessed | tf_op | source)
XLA Modules:
  0.0 383.9 jit_solution(1197257132475756715)
XLA Ops:
  13.0 10.0 %all-gather = f32[256,256]{1,0:T(8,128)S(1)} all-gather(f32[64,256]{1,0:T(8,128)S(1)} %slice_add_fusion.1), channel_id=2, replica_groups=mesh['leaf'=8,'sub'=4] {'sub'}, dimensions={0}, use_global_device_ids=true | all-gather | bytes 327680 | tf_op jit(solution)/shard_map/all_gather | solution.py:28
  27.6 12.5 %all_gather.20 = f32[256,768]{1,0:T(8,128)S(1)} all-gather(f32[64,768]{1,0:T(8,128)S(1)} %slice.143), channel_id=1, replica_groups=mesh['leaf'=8,'sub'=4] {'sub'}, dimensions={0}, use_global_device_ids=true | all-gather | bytes 983040 | tf_op jit(solution)/shard_map/all_gather | solution.py:60
  40.0 10.2 %all_gather.19 = f32[256,768]{1,0:T(8,128)S(1)} all-gather(f32[64,768]{1,0:T(8,128)S(1)} %slice.142), channel_id=1, replica_groups=mesh['leaf'=8,'sub'=4] {'sub'}, dimensions={0}, use_global_device_ids=true | all-gather | bytes 983040 | tf_op jit(solution)/shard_map/all_gather | solution.py:59
  50.6 1.2 convolution_subtract_fusion
  51.8 1.5 reshape_reshape.3
  53.3 2.8 copy.20
  56.1 1.9 gather_fusion.3
  59.1 2.3 collective-permute-done.1
  61.4 1.0 fusion.90
  62.4 1.6 collective-permute-start.2
  64.0 18.3 %collective-permute-done.2 = f32[2,64,1536]{2,1,0:T(8,128)} collective-permute-done((f32[2,64,1536]{2,1,0:T(8,128)}, f32[2,64,1536]{2,1,0:T(8,128)}, u32[]{:S(2)}, u32[]{:S(2)}) %collective-permute-start.2) | collective-permute-done | bytes 786464 | tf_op jit(solution)/shard_map/ppermute | solution.py:14
  82.3 1.5 broadcast_select_fusion.3
  85.5 1.9 slice.148
  95.5 16.9 %all-gather.5.cloned.1.call-done = f32[2,256,512]{2,1,0:T(8,128)} async-done(((f32[2,64,512]{2,1,0:T(8,128)}), f32[2,256,512]{2,1,0:T(8,128)}) %all-gather.5.cloned.1.call-update) | async-done | bytes 1048592 | tf_op jit(solution)/shard_map/all_gather | solution.py:28
  112.4 1.4 abs_reduce_fusion
  115.1 3.1 fusion.2
  118.2 1.8 fusion.7
  120.0 1.8 fusion.45
  121.8 1.8 convolution_subtract_fusion.4
  123.7 1.8 fusion.46
  125.6 1.8 convolution_subtract_fusion.3
  127.4 2.1 fusion.47
  129.5 1.9 convolution_subtract_fusion.2
  132.3 17.2 %all-gather.7.cloned.1.call-done = f32[2,256,1024]{2,1,0:T(8,128)} async-done(((f32[2,64,1024]{2,1,0:T(8,128)}), f32[2,256,1024]{2,1,0:T(8,128)}) %all-gather.7.cloned.1.call-update) | async-done | bytes 2097168 | tf_op jit(solution)/shard_map/all_gather | solution.py:103
  149.5 3.2 constant_dynamic-update-slice_fusion.1
  152.7 34.4 %all-gather.9.cloned.1.call-done = f32[2,256,1024]{2,1,0:T(8,128)} async-done(((f32[2,64,1024]{2,1,0:T(8,128)}), f32[2,256,1024]{2,1,0:T(8,128)}) %all-gather.9.cloned.1.call-update) | async-done | bytes 2097168 | tf_op jit(solution)/shard_map/all_gather | solution.py:104
  187.1 3.2 constant_dynamic-update-slice_fusion
  190.3 7.3 %copy.24 = f32[2,256,2048]{1,0,2:T(2,128)} copy(f32[2,256,2048]{2,1,0:T(8,128)} %constant_dynamic-update-slice_fusion) | data formatting | bytes 8388608 | tf_op jit(solution)/shard_map/reshape | solution.py:110
  197.6 1.0 constant_dynamic-slice_fusion.1
  198.7 1.4 fusion.49
  200.2 4.7 %convolution_subtract_fusion.1 = f32[192,2048]{1,0:T(8,128)S(1)} fusion(f32[192,512]{1,0:T(8,128)S(1)} %fusion.48, f32[512,2048]{1,0:T(8,128)} %bitcast.129, f32[192,1024]{1,0:T(8,128)S(1)} %bitcast.131, pred[]{:T(512)S(6)} %eq.94), kind=kOutput, calls=%fused_computation.8 | convolution fusion | flops 2416705536 | bytes 6946817 | tf_op jit(solution)/shard_map/dot_general | solution.py:18
  205.8 39.8 %all-reduce.7.cloned.1.call-done = f32[512,256]{1,0:T(8,128)} async-done(((f32[512,256]{1,0:T(8,128)}), f32[512,256]{1,0:T(8,128)}) %all-reduce.7.cloned.1.call-update) | async-done | bytes 524304 | tf_op jit(solution)/shard_map/psum | solution.py:137
  245.6 1.8 multiply_add_fusion
  247.5 1.5 constant_dynamic-slice_fusion.3
  250.0 1.5 collective-permute-start.3
  251.5 1.6 add_dynamic-update-slice_fusion
  254.5 1.5 collective-permute-start.8
  257.0 1.4 copy.23
  258.4 51.7 %collective-permute-done.6 = f32[8,64,256]{2,1,0:T(8,128)} collective-permute-done((f32[8,64,256]{2,1,0:T(8,128)}, f32[8,64,256]{2,1,0:T(8,128)}, u32[]{:S(2)}, u32[]{:S(2)}) %collective-permute-start.6) | collective-permute-done | bytes 524320 | tf_op jit(solution)/shard_map/ppermute | solution.py:14
  310.1 1.1 dynamic-slice_add_fusion.2
  311.1 9.7 %collective-permute-done.8 = f32[512,256]{1,0:T(8,128)} collective-permute-done((f32[512,256]{1,0:T(8,128)}, f32[512,256]{1,0:T(8,128)}, u32[]{:S(2)}, u32[]{:S(2)}) %collective-permute-start.8) | collective-permute-done | bytes 524320 | tf_op jit(solution)/shard_map/ppermute | solution.py:14
  320.9 2.2 convolution_negate_fusion
  323.8 1.4 convolution_bitcast_fusion
  325.3 43.1 %all-reduce.9.cloned.1.call-done = f32[256,256]{1,0:T(8,128)} async-done(((f32[256,256]{1,0:T(8,128)}), f32[256,256]{1,0:T(8,128)}) %all-reduce.9.cloned.1.call-update) | async-done | bytes 262160 | tf_op jit(solution)/shard_map/psum | solution.py:154
  368.4 2.5 dynamic-slice_add_fusion
  370.9 1.0 constant_dynamic-slice_fusion.2
  372.5 1.5 fusion.18
  375.1 2.3 dynamic-slice_add_fusion.1
  (119 shorter events, 24.9 us)
Async XLA Ops:
  7.2 1.2 copy-start
  7.2 105.2 %all-gather.5.cloned.1.call-start = ((), (), s32[]{:S(2)}) async-start(), calls=%async_computation | async-start | bytes 1310720 | tf_op jit(solution)/shard_map/all_gather | solution.py:28
  10.3 2.6 collective-permute-start
  26.8 23.8 %copy-start.8 = (f32[3,64,768]{2,1,0:T(8,128)S(1)}, f32[3,64,768]{2,1,0:T(8,128)}, u32[]{:S(2)}) copy-start(f32[3,64,768]{2,1,0:T(8,128)} %slice.137) | copy-start | bytes 1769476
  50.2 1.6 copy-start.5
  58.3 37.3 %copy-start.4 = (f32[3,64,1536]{2,1,0:T(8,128)}, f32[3,64,1536]{2,1,0:T(8,128)S(1)}, u32[]{:S(2)}) copy-start(f32[3,64,1536]{2,1,0:T(8,128)S(1)} %broadcast_select_fusion) | copy-start | bytes 3538948
  59.0 2.4 collective-permute-start.1
  62.4 19.9 %collective-permute-start.2 = (f32[2,64,1536]{2,1,0:T(8,128)}, f32[2,64,1536]{2,1,0:T(8,128)}, u32[]{:S(2)}, u32[]{:S(2)}) collective-permute-start(f32[2,64,1536]{2,1,0:T(8,128)} %fusion.90), channel_id=1, source_target_pairs={{0,8},{4,12},{8,0},{12,4},{16,24},{20,28},{24,16},{28,20},{1,9},{5... | collective-permute-start | bytes 2359304 | tf_op jit(solution)/shard_map/ppermute | solution.py:14
  83.8 0.9 copy-start.7
  83.8 4.5 %copy-start.9 = (f32[2,64,256]{2,1,0:T(8,128)S(1)}, f32[2,64,256]{2,1,0:T(8,128)}, u32[]{:S(2)}) copy-start(f32[2,64,256]{2,1,0:T(8,128)} %param.7) | copy-start | bytes 393220
  85.5 64.0 %all-gather.7.cloned.1.call-start = ((), (), s32[]{:S(2)}) async-start(), calls=%async_computation.1 | async-start | bytes 2621440 | tf_op jit(solution)/shard_map/all_gather | solution.py:103
  87.5 99.7 %all-gather.9.cloned.1.call-start = ((), (), s32[]{:S(2)}) async-start(), calls=%async_computation.2 | async-start | bytes 2621440 | tf_op jit(solution)/shard_map/all_gather | solution.py:104
  89.0 162.5 %collective-permute-start.5 = (f32[8,64,256]{2,1,0:T(8,128)}, f32[8,64,256]{2,1,0:T(8,128)}, u32[]{:S(2)}, u32[]{:S(2)}) collective-permute-start(f32[8,64,256]{2,1,0:T(8,128)} %constant_dynamic-update-slice_fusion.2), channel_id=1, source_target_pairs={{0,4},{4,0},{8,12},{12,8},{16,20},{20,16},{24,28},{28,24},{1,5},{5... | collective-permute-start | bytes 1572872 | tf_op jit(solution)/shard_map/ppermute | solution.py:14
  95.3 150.4 %all-reduce.7.cloned.1.call-start = ((), (), s32[]{:S(2)}) async-start(), calls=%async_computation.3 | async-start | bytes 1048576 | tf_op jit(solution)/shard_map/psum | solution.py:137
  115.1 4.9 %copy-start.2 = (f32[2,256,512]{2,1,0:T(8,128)S(1)}, f32[2,256,512]{2,1,0:T(8,128)}, u32[]{:S(2)}) copy-start(f32[2,256,512]{2,1,0:T(8,128)} %all-gather.5.cloned.1.call-done) | copy-start | bytes 3145732
  129.5 1.9 slice-start
  197.6 2.6 slice-start.1
  200.1 168.3 %all-reduce.9.cloned.1.call-start = ((), (), s32[]{:S(2)}) async-start(), calls=%async_computation.4 | async-start | bytes 524288 | tf_op jit(solution)/shard_map/psum | solution.py:154
  245.6 8.0 %collective-permute-start.7 = (f32[512,256]{1,0:T(8,128)}, f32[512,256]{1,0:T(8,128)S(1)}, u32[]{:S(2)}, u32[]{:S(2)}) collective-permute-start(f32[512,256]{1,0:T(8,128)} %all-reduce.7.cloned.1.call-done), channel_id=1, source_target_pairs={{0,4},{4,0},{8,12},{12,8},{16,20},{20,16},{24,28},{28,24},{1,5},{5... | collective-permute-start | bytes 1572872 | tf_op jit(solution)/shard_map/ppermute | solution.py:14
  247.4 2.6 copy-start.3
  247.5 6.2 %copy-start.10 = (f32[512,256]{1,0:T(8,128)S(1)}, f32[512,256]{1,0:T(8,128)}, u32[]{:S(2)}) copy-start(f32[512,256]{1,0:T(8,128)} %all-reduce.7.cloned.1.call-done) | copy-start | bytes 1572868
  247.5 8.5 %copy-start.6 = (f32[256,768]{1,0:T(8,128)S(1)}, f32[256,768]{1,0:T(8,128)}, u32[]{:S(2)}) copy-start(f32[256,768]{1,0:T(8,128)} %copy-done.5) | copy-start | bytes 2359300
  250.0 118.4 %collective-permute-start.3 = (f32[4,64,2048]{2,1,0:T(8,128)}, f32[4,64,2048]{2,1,0:T(8,128)}, u32[]{:S(2)}, u32[]{:S(2)}) collective-permute-start(f32[4,64,2048]{2,1,0:T(8,128)} %constant_dynamic-slice_fusion.3), channel_id=1, source_target_pairs={{0,8},{4,12},{8,0},{12,4},{16,24},{20,28},{24,16},{28,20},{1,9},{5... | collective-permute-start | bytes 6291464 | tf_op jit(solution)/shard_map/ppermute | solution.py:14
  253.1 57.0 %collective-permute-start.6 = (f32[8,64,256]{2,1,0:T(8,128)}, f32[8,64,256]{2,1,0:T(8,128)}, u32[]{:S(2)}, u32[]{:S(2)}) collective-permute-start(f32[8,64,256]{2,1,0:T(8,128)} %add_dynamic-update-slice_fusion), channel_id=1, source_target_pairs={{0,8},{4,12},{8,0},{12,4},{16,24},{20,28},{24,16},{28,20},{1,9},{5... | collective-permute-start | bytes 1572872 | tf_op jit(solution)/shard_map/ppermute | solution.py:14
  254.5 66.3 %collective-permute-start.8 = (f32[512,256]{1,0:T(8,128)}, f32[512,256]{1,0:T(8,128)}, u32[]{:S(2)}, u32[]{:S(2)}) collective-permute-start(f32[512,256]{1,0:T(8,128)} %add.281), channel_id=1, source_target_pairs={{0,8},{4,12},{8,0},{12,4},{16,24},{20,28},{24,16},{28,20},{1,9},{5... | collective-permute-start | bytes 1572872 | tf_op jit(solution)/shard_map/ppermute | solution.py:14
  368.4 4.1 %collective-permute-start.9 = (f32[256,256]{1,0:T(8,128)}, f32[256,256]{1,0:T(8,128)}, u32[]{:S(2)}, u32[]{:S(2)}) collective-permute-start(f32[256,256]{1,0:T(8,128)} %all-reduce.9.cloned.1.call-done), channel_id=1, source_target_pairs={{0,4},{4,0},{8,12},{12,8},{16,20},{20,16},{24,28},{28,24},{1,5},{5... | collective-permute-start | bytes 786440 | tf_op jit(solution)/shard_map/ppermute | solution.py:14
  371.9 3.1 collective-permute-start.4
  372.5 4.9 %copy-start.1 = (f32[4,64,1024]{2,1,0:T(8,128)S(1)}, f32[4,64,1024]{2,1,0:T(8,128)}, u32[]{:S(2)}) copy-start(f32[4,64,1024]{2,1,0:T(8,128)} %param.4) | copy-start | bytes 3145732
Sparse Core Ops, SparseCore 0:
  85.6 26.7 all-gather.4
  114.3 35.1 all-gather.6
  151.9 35.1 all-gather.8
  200.2 45.3 all-reduce.6
  325.3 43.0 all-reduce.8
where the time goes:
time: 385 us; the launch traced here: 384 us
  waiting for transfers between devices  234 us (61%)
  local copies, waits for them, and re-layouts  38.4 us (10%)
  matrix products  32.8 us (9%)
  blocking collectives  32.7 us (8%)
  other arithmetic  19.8 us (5%)
  between operations  19.8 us (5%)
  starting transfers between devices  6.62 us (2%)
    ppermute x10, waiting for transfers between devices, swapped(): return lax.ppermute(value, axis, pairs)  82.2 us
    psum x1, waiting for transfers between devices, shards(): partial_one = lax.psum(partial_one, 'sub')  43.1 us
    psum x1, waiting for transfers between devices, shards(): partial_two = lax.psum(partial_two, 'sub')  39.8 us
    all_gather x1, waiting for transfers between devices, shards(): lax.all_gather(second_node[:, :, :4 * W], 'sub', axis=1, tiled=True)  34.4 us
    dot_general x24, matrix products, exact_dot(): jnp.dot(left_matrix, right_matrix, precision=lax.Precision.HIGHEST, prefe...  32.8 us
    all_gather x1, waiting for transfers between devices, shards(): lax.all_gather(first_node[:, :, :4 * W], 'sub', axis=1, tiled=True)  17.2 us
    all_gather x1, waiting for transfers between devices, interface_inverse(): lax.all_gather(block_rows, 'sub', axis=1, tiled=True)  16.9 us
    all_gather x1, blocking collectives, shards(): lax.all_gather(second_piece[:, :3 * W], 'sub', axis=0, tiled=True)  12.5 us
  transfers between devices with their start and end apart: 15, of which 10 were waited for; matrix products, arithmetic and copies ran while one was open for 18% of the time, Pallas kernels for 0%

commit v1 on v0

--- a/solution.py
+++ b/solution.py
@@ -6,6 +6,16 @@
 W = 256
 K = 256
 NS_STEPS = 4
+
+
+def gather_around(x, axis, dim):
+    ways, here, step = (lax.axis_size(axis), lax.axis_index(axis), x.shape[dim])
+    shape = [n * ways if d == dim else n for d, n in enumerate(x.shape)]
+    full = lax.dynamic_update_slice_in_dim(jnp.zeros(shape, x.dtype), x, here * step, axis=dim)
+    for far in range(1, ways):
+        x = lax.ppermute(x, axis, [(d, (d + 1) % ways) for d in range(ways)])
+        full = lax.dynamic_update_slice_in_dim(full, x, (here - far) % ways * step, axis=dim)
+    return full
 
 
 def swapped(value, axis, apart):
@@ -25,9 +35,7 @@
 
 def interface_inverse(block_rows):
     slot_count, width_local, block_size = block_rows.shape
-    full_block = lax.all_gather(block_rows, "sub", axis=1, tiled=True).reshape(
-        block_size, block_size
-    )
+    full_block = gather_around(block_rows, "sub", 1).reshape(block_size, block_size)
     row_bound = jnp.max(jnp.sum(jnp.abs(full_block), axis=1))
     iterate = jnp.eye(block_size, dtype=jnp.float32) / row_bound
     for iteration in range(NS_STEPS):

time: 385 us -> 369 us (0.958)
  waiting for transfers between devices: 234 us -> 215 us
  starting transfers between devices: 6.62 us -> 17.3 us
  blocking collectives: 32.7 us -> 23 us
    ppermute x0 -> x6, waiting for transfers between devices: none -> 28.4 us  [gather_around(): x = lax.ppermute(x, axis, [(d, (d + 1) % ways) for d in range(ways)])]
    all_gather x1, waiting for transfers between devices: 17.2 us -> 0.02 us  [shards(): lax.all_gather(first_node[:, :, :4 * W], 'sub', axis=1, tiled=True)]
    all_gather x1 -> x0, waiting for transfers between devices: 16.9 us -> none  [interface_inverse(): lax.all_gather(block_rows, 'sub', axis=1, tiled=True)]
    all_gather x1, waiting for transfers between devices: 34.4 us -> 21.1 us  [shards(): lax.all_gather(second_node[:, :, :4 * W], 'sub', axis=1, tiled=True)]
    ppermute x0 -> x6, starting transfers between devices: none -> 10.7 us  [gather_around(): x = lax.ppermute(x, axis, [(d, (d + 1) % ways) for d in range(ways)])]
    all_gather x1 -> x0, blocking collectives: 10 us -> none  [interface_inverse(): lax.all_gather(block_rows, 'sub', axis=1, tiled=True)]
  transfers between devices with their start and end apart: 15 -> 20, of which waited for: 10 -> 13; matrix products, arithmetic and copies ran while one was open for 18% -> 19% of each run, Pallas kernels for 0% -> 0%
where the time goes in v1:
time: 369 us; the launch traced here: 368 us
  waiting for transfers between devices  215 us (58%)
  local copies, waits for them, and re-layouts  41.1 us (11%)
  matrix products  31.5 us (9%)
  blocking collectives  23 us (6%)
  other arithmetic  20.5 us (6%)
  between operations  19.5 us (5%)
  starting transfers between devices  17.3 us (5%)
    ppermute x10, waiting for transfers between devices, swapped(): return lax.ppermute(value, axis, pairs)  82.2 us
    psum x1, waiting for transfers between devices, shards(): partial_one = lax.psum(partial_one, 'sub')  43.1 us
    psum x1, waiting for transfers between devices, shards(): partial_two = lax.psum(partial_two, 'sub')  39.8 us
    dot_general x24, matrix products, exact_dot(): jnp.dot(left_matrix, right_matrix, precision=lax.Precision.HIGHEST, prefe...  31.5 us
    ppermute x6, waiting for transfers between devices, gather_around(): x = lax.ppermute(x, axis, [(d, (d + 1) % ways) for d in range(ways)])  28.4 us
    all_gather x1, waiting for transfers between devices, shards(): lax.all_gather(second_node[:, :, :4 * W], 'sub', axis=1, tiled=True)  21.1 us
    all_gather x1, blocking collectives, shards(): lax.all_gather(second_piece[:, :3 * W], 'sub', axis=0, tiled=True)  12.1 us
    all_gather x1, blocking collectives, shards(): lax.all_gather(first_piece[:, :3 * W], 'sub', axis=0, tiled=True)  10.9 us
  transfers between devices with their start and end apart: 20, of which 13 were waited for; matrix products, arithmetic and copies ran while one was open for 19% of the time, Pallas kernels for 0%

profile of v1, /device:TPU:0, one launch (start us, length us, event | category | flops | bytes accessed | tf_op | source)
XLA Modules:
  0.0 367.7 jit_solution(17693430087423847383)
XLA Ops:
  13.1 2.6 collective-permute-start.1
  15.7 12.1 %all_gather.13 = f32[256,768]{1,0:T(8,128)S(1)} all-gather(f32[64,768]{1,0:T(8,128)S(1)} %slice.143), channel_id=1, replica_groups=mesh['leaf'=8,'sub'=4] {'sub'}, dimensions={0}, use_global_device_ids=true | all-gather | bytes 983040 | tf_op jit(solution)/shard_map/all_gather | solution.py:68
  27.8 10.9 %all_gather.12 = f32[256,768]{1,0:T(8,128)S(1)} all-gather(f32[64,768]{1,0:T(8,128)S(1)} %slice.142), channel_id=1, replica_groups=mesh['leaf'=8,'sub'=4] {'sub'}, dimensions={0}, use_global_device_ids=true | all-gather | bytes 983040 | tf_op jit(solution)/shard_map/all_gather | solution.py:67
  38.7 2.5 collective-permute-start.2
  41.2 2.6 collective-permute-done.2
  43.8 1.6 collective-permute-start.3
  45.5 3.5 collective-permute-done.3
  55.1 1.5 reshape_reshape.3
  56.6 2.8 copy.22
  59.4 1.9 gather_fusion.3
  62.4 2.3 collective-permute-done.4
  65.7 1.6 collective-permute-start.5
  67.3 18.3 %collective-permute-done.5 = f32[2,64,1536]{2,1,0:T(8,128)} collective-permute-done((f32[2,64,1536]{2,1,0:T(8,128)}, f32[2,64,1536]{2,1,0:T(8,128)}, u32[]{:S(2)}, u32[]{:S(2)}) %collective-permute-start.5) | collective-permute-done | bytes 786464 | tf_op jit(solution)/shard_map/ppermute | solution.py:24
  85.6 2.4 broadcast_select_fusion.3
  90.6 1.8 constant_dynamic-update-slice_fusion.4
  93.9 9.6 %collective-permute-done.6 = f32[2,64,512]{2,1,0:T(8,128)} collective-permute-done((f32[2,64,512]{2,1,0:T(8,128)}, f32[2,64,512]{2,1,0:T(8,128)}, u32[]{:S(2)}, u32[]{:S(2)}) %collective-permute-start.6) | collective-permute-done | bytes 262176 | tf_op jit(solution)/shard_map/ppermute | solution.py:16
  103.5 2.6 collective-permute-start.7
  110.4 3.2 collective-permute-done.7
  118.6 9.5 %collective-permute-done.8 = f32[2,64,512]{2,1,0:T(8,128)} collective-permute-done((f32[2,64,512]{2,1,0:T(8,128)}, f32[2,64,512]{2,1,0:T(8,128)}, u32[]{:S(2)}, u32[]{:S(2)}) %collective-permute-start.8) | collective-permute-done | bytes 262176 | tf_op jit(solution)/shard_map/ppermute | solution.py:16
  130.6 1.8 fusion.2
  132.4 1.8 fusion.7
  134.2 1.8 fusion.47
  136.0 1.9 convolution_subtract_fusion.4
  137.9 1.9 fusion.48
  139.7 1.8 convolution_subtract_fusion.3
  141.6 2.1 fusion.49
  143.7 1.9 convolution_subtract_fusion.2
  146.5 3.3 constant_dynamic-update-slice_fusion.6
  149.7 21.1 %all-gather.5.cloned.1.call-done = f32[2,256,1024]{2,1,0:T(8,128)} async-done(((f32[2,64,1024]{2,1,0:T(8,128)}), f32[2,256,1024]{2,1,0:T(8,128)}) %all-gather.5.cloned.1.call-update) | async-done | bytes 2097168 | tf_op jit(solution)/shard_map/all_gather | solution.py:112
  170.8 3.3 constant_dynamic-update-slice_fusion.5
  174.1 7.3 %copy.26 = f32[2,256,2048]{1,0,2:T(2,128)} copy(f32[2,256,2048]{2,1,0:T(8,128)} %constant_dynamic-update-slice_fusion.5) | data formatting | bytes 8388608 | tf_op jit(solution)/shard_map/reshape | solution.py:118
  182.5 1.4 fusion.51
  184.0 4.7 %convolution_subtract_fusion.1 = f32[192,2048]{1,0:T(8,128)S(1)} fusion(f32[192,512]{1,0:T(8,128)S(1)} %fusion.50, f32[512,2048]{1,0:T(8,128)} %bitcast.137, f32[192,1024]{1,0:T(8,128)S(1)} %bitcast.139, pred[]{:T(512)S(6)} %eq.100), kind=kOutput, calls=%fused_computation.8 | convolution fusion | flops 2416705536 | bytes 6946817 | tf_op jit(solution)/shard_map/dot_general | solution.py:28
  189.6 39.8 %all-reduce.7.cloned.1.call-done = f32[512,256]{1,0:T(8,128)} async-done(((f32[512,256]{1,0:T(8,128)}), f32[512,256]{1,0:T(8,128)}) %all-reduce.7.cloned.1.call-update) | async-done | bytes 524304 | tf_op jit(solution)/shard_map/psum | solution.py:145
  229.5 1.8 multiply_add_fusion
  231.3 1.5 constant_dynamic-slice_fusion.3
  233.9 1.5 collective-permute-start.9
  235.3 1.6 add_dynamic-update-slice_fusion
  238.3 1.5 collective-permute-start.14
  240.9 1.4 copy.25
  242.3 51.7 %collective-permute-done.12 = f32[8,64,256]{2,1,0:T(8,128)} collective-permute-done((f32[8,64,256]{2,1,0:T(8,128)}, f32[8,64,256]{2,1,0:T(8,128)}, u32[]{:S(2)}, u32[]{:S(2)}) %collective-permute-start.12) | collective-permute-done | bytes 524320 | tf_op jit(solution)/shard_map/ppermute | solution.py:24
  295.0 9.7 %collective-permute-done.14 = f32[512,256]{1,0:T(8,128)} collective-permute-done((f32[512,256]{1,0:T(8,128)}, f32[512,256]{1,0:T(8,128)}, u32[]{:S(2)}, u32[]{:S(2)}) %collective-permute-start.14) | collective-permute-done | bytes 524320 | tf_op jit(solution)/shard_map/ppermute | solution.py:24
  304.7 2.2 convolution_negate_fusion
  307.6 1.4 convolution_bitcast_fusion
  309.1 43.1 %all-reduce.9.cloned.1.call-done = f32[256,256]{1,0:T(8,128)} async-done(((f32[256,256]{1,0:T(8,128)}), f32[256,256]{1,0:T(8,128)}) %all-reduce.9.cloned.1.call-update) | async-done | bytes 262160 | tf_op jit(solution)/shard_map/psum | solution.py:162
  352.2 2.5 dynamic-slice_add_fusion
  356.3 1.5 fusion.18
  358.9 2.3 dynamic-slice_add_fusion.1
  (135 shorter events, 35.5 us)
Async XLA Ops:
  7.2 1.2 copy-start
  7.2 139.3 %all-gather.3.cloned.1.call-start = ((), (), s32[]{:S(2)}) async-start(), calls=%async_computation | async-start | bytes 2621440 | tf_op jit(solution)/shard_map/all_gather | solution.py:111
  10.3 2.7 collective-permute-start
  13.1 25.5 %collective-permute-start.1 = (f32[1,64,256]{2,1,0:T(8,128)S(1)}, f32[1,64,256]{2,1,0:T(8,128)S(1)}, u32[]{:S(2)}, u32[]{:S(2)}) collective-permute-start(f32[1,64,256]{2,1,0:T(8,128)S(1)} %get-tuple-element.13), channel_id=1, source_target_pairs={{0,1},{1,2},{2,3},{3,0},{4,5},{5,6},{6,7},{7,4},{8,9},{9,10},{10,1... | collective-permute-start | bytes 196616 | tf_op jit(solution)/shard_map/ppermute | solution.py:16
  38.7 15.2 %copy-start.4 = (f32[256,768]{1,0:T(8,128)}, f32[256,768]{1,0:T(8,128)S(1)}, u32[]{:S(2)}) copy-start(f32[256,768]{1,0:T(8,128)S(1)} %all_gather.12) | copy-start | bytes 2359300
  38.7 5.2 %collective-permute-start.2 = (f32[1,64,256]{2,1,0:T(8,128)S(1)}, f32[1,64,256]{2,1,0:T(8,128)S(1)}, u32[]{:S(2)}, u32[]{:S(2)}) collective-permute-start(f32[1,64,256]{2,1,0:T(8,128)S(1)} %collective-permute-done.1), channel_id=1, source_target_pairs={{0,1},{1,2},{2,3},{3,0},{4,5},{5,6},{6,7},{7,4},{8,9},{9,10},{10,1... | collective-permute-start | bytes 196616 | tf_op jit(solution)/shard_map/ppermute | solution.py:16
  43.8 5.2 %collective-permute-start.3 = (f32[1,64,256]{2,1,0:T(8,128)S(1)}, f32[1,64,256]{2,1,0:T(8,128)S(1)}, u32[]{:S(2)}, u32[]{:S(2)}) collective-permute-start(f32[1,64,256]{2,1,0:T(8,128)S(1)} %collective-permute-done.2), channel_id=1, source_target_pairs={{0,1},{1,2},{2,3},{3,0},{4,5},{5,6},{6,7},{7,4},{8,9},{9,10},{10,1... | collective-permute-start | bytes 196616 | tf_op jit(solution)/shard_map/ppermute | solution.py:16
  52.0 1.9 copy-start.8
  61.6 52.7 %copy-start.3 = (f32[3,64,1536]{2,1,0:T(8,128)}, f32[3,64,1536]{2,1,0:T(8,128)S(1)}, u32[]{:S(2)}) copy-start(f32[3,64,1536]{2,1,0:T(8,128)S(1)} %broadcast_select_fusion) | copy-start | bytes 3538948
  62.3 2.4 collective-permute-start.4
  65.7 19.9 %collective-permute-start.5 = (f32[2,64,1536]{2,1,0:T(8,128)}, f32[2,64,1536]{2,1,0:T(8,128)}, u32[]{:S(2)}, u32[]{:S(2)}) collective-permute-start(f32[2,64,1536]{2,1,0:T(8,128)} %fusion.92), channel_id=1, source_target_pairs={{0,8},{4,12},{8,0},{12,4},{16,24},{20,28},{24,16},{28,20},{1,9},{5... | collective-permute-start | bytes 2359304 | tf_op jit(solution)/shard_map/ppermute | solution.py:24
  67.3 22.5 %copy-start.9 = (f32[2,64,256]{2,1,0:T(8,128)S(1)}, f32[2,64,256]{2,1,0:T(8,128)}, u32[]{:S(2)}) copy-start(f32[2,64,256]{2,1,0:T(8,128)} %param.7) | copy-start | bytes 393220
  88.0 2.5 copy-start.7
  88.9 81.9 %all-gather.5.cloned.1.call-start = ((), (), s32[]{:S(2)}) async-start(), calls=%async_computation.1 | async-start | bytes 2621440 | tf_op jit(solution)/shard_map/all_gather | solution.py:112
  90.5 144.9 %collective-permute-start.11 = (f32[8,64,256]{2,1,0:T(8,128)}, f32[8,64,256]{2,1,0:T(8,128)}, u32[]{:S(2)}, u32[]{:S(2)}) collective-permute-start(f32[8,64,256]{2,1,0:T(8,128)} %constant_dynamic-update-slice_fusion), channel_id=1, source_target_pairs={{0,4},{4,0},{8,12},{12,8},{16,20},{20,16},{24,28},{28,24},{1,5},{5... | collective-permute-start | bytes 1572872 | tf_op jit(solution)/shard_map/ppermute | solution.py:24
  92.4 11.1 %collective-permute-start.6 = (f32[2,64,512]{2,1,0:T(8,128)}, f32[2,64,512]{2,1,0:T(8,128)}, u32[]{:S(2)}, u32[]{:S(2)}) collective-permute-start(f32[2,64,512]{2,1,0:T(8,128)} %get-tuple-element.5), channel_id=1, source_target_pairs={{0,1},{1,2},{2,3},{3,0},{4,5},{5,6},{6,7},{7,4},{8,9},{9,10},{10,1... | collective-permute-start | bytes 786440 | tf_op jit(solution)/shard_map/ppermute | solution.py:16
  103.5 10.1 %collective-permute-start.7 = (f32[2,64,512]{2,1,0:T(8,128)}, f32[2,64,512]{2,1,0:T(8,128)}, u32[]{:S(2)}, u32[]{:S(2)}) collective-permute-start(f32[2,64,512]{2,1,0:T(8,128)} %collective-permute-done.6), channel_id=1, source_target_pairs={{0,1},{1,2},{2,3},{3,0},{4,5},{5,6},{6,7},{7,4},{8,9},{9,10},{10,1... | collective-permute-start | bytes 786440 | tf_op jit(solution)/shard_map/ppermute | solution.py:16
  113.6 14.6 %collective-permute-start.8 = (f32[2,64,512]{2,1,0:T(8,128)}, f32[2,64,512]{2,1,0:T(8,128)}, u32[]{:S(2)}, u32[]{:S(2)}) collective-permute-start(f32[2,64,512]{2,1,0:T(8,128)} %collective-permute-done.7), channel_id=1, source_target_pairs={{0,1},{1,2},{2,3},{3,0},{4,5},{5,6},{6,7},{7,4},{8,9},{9,10},{10,1... | collective-permute-start | bytes 786440 | tf_op jit(solution)/shard_map/ppermute | solution.py:16
  114.2 1.4 copy-start.6
  116.4 113.0 %all-reduce.7.cloned.1.call-start = ((), (), s32[]{:S(2)}) async-start(), calls=%async_computation.2 | async-start | bytes 1048576 | tf_op jit(solution)/shard_map/psum | solution.py:145
  143.7 1.9 slice-start
  181.4 2.6 slice-start.1
  183.9 168.3 %all-reduce.9.cloned.1.call-start = ((), (), s32[]{:S(2)}) async-start(), calls=%async_computation.3 | async-start | bytes 524288 | tf_op jit(solution)/shard_map/psum | solution.py:162
  229.5 8.0 %collective-permute-start.13 = (f32[512,256]{1,0:T(8,128)}, f32[512,256]{1,0:T(8,128)S(1)}, u32[]{:S(2)}, u32[]{:S(2)}) collective-permute-start(f32[512,256]{1,0:T(8,128)} %all-reduce.7.cloned.1.call-done), channel_id=1, source_target_pairs={{0,4},{4,0},{8,12},{12,8},{16,20},{20,16},{24,28},{28,24},{1,5},{5... | collective-permute-start | bytes 1572872 | tf_op jit(solution)/shard_map/ppermute | solution.py:24
  231.3 2.6 copy-start.2
  231.3 6.2 %copy-start.10 = (f32[512,256]{1,0:T(8,128)S(1)}, f32[512,256]{1,0:T(8,128)}, u32[]{:S(2)}) copy-start(f32[512,256]{1,0:T(8,128)} %all-reduce.7.cloned.1.call-done) | copy-start | bytes 1572868
  231.3 8.6 %copy-start.5 = (f32[256,768]{1,0:T(8,128)S(1)}, f32[256,768]{1,0:T(8,128)}, u32[]{:S(2)}) copy-start(f32[256,768]{1,0:T(8,128)} %copy-done.4) | copy-start | bytes 2359300
  233.9 118.4 %collective-permute-start.9 = (f32[4,64,2048]{2,1,0:T(8,128)}, f32[4,64,2048]{2,1,0:T(8,128)}, u32[]{:S(2)}, u32[]{:S(2)}) collective-permute-start(f32[4,64,2048]{2,1,0:T(8,128)} %constant_dynamic-slice_fusion.3), channel_id=1, source_target_pairs={{0,8},{4,12},{8,0},{12,4},{16,24},{20,28},{24,16},{28,20},{1,9},{5... | collective-permute-start | bytes 6291464 | tf_op jit(solution)/shard_map/ppermute | solution.py:24
  236.9 57.0 %collective-permute-start.12 = (f32[8,64,256]{2,1,0:T(8,128)}, f32[8,64,256]{2,1,0:T(8,128)}, u32[]{:S(2)}, u32[]{:S(2)}) collective-permute-start(f32[8,64,256]{2,1,0:T(8,128)} %add_dynamic-update-slice_fusion), channel_id=1, source_target_pairs={{0,8},{4,12},{8,0},{12,4},{16,24},{20,28},{24,16},{28,20},{1,9},{5... | collective-permute-start | bytes 1572872 | tf_op jit(solution)/shard_map/ppermute | solution.py:24
  238.3 66.3 %collective-permute-start.14 = (f32[512,256]{1,0:T(8,128)}, f32[512,256]{1,0:T(8,128)}, u32[]{:S(2)}, u32[]{:S(2)}) collective-permute-start(f32[512,256]{1,0:T(8,128)} %add.316), channel_id=1, source_target_pairs={{0,8},{4,12},{8,0},{12,4},{16,24},{20,28},{24,16},{28,20},{1,9},{5... | collective-permute-start | bytes 1572872 | tf_op jit(solution)/shard_map/ppermute | solution.py:24
  352.2 4.1 %collective-permute-start.15 = (f32[256,256]{1,0:T(8,128)}, f32[256,256]{1,0:T(8,128)}, u32[]{:S(2)}, u32[]{:S(2)}) collective-permute-start(f32[256,256]{1,0:T(8,128)} %all-reduce.9.cloned.1.call-done), channel_id=1, source_target_pairs={{0,4},{4,0},{8,12},{12,8},{16,20},{20,16},{24,28},{28,24},{1,5},{5... | collective-permute-start | bytes 786440 | tf_op jit(solution)/shard_map/ppermute | solution.py:24
  355.8 3.1 collective-permute-start.10
  356.3 4.9 %copy-start.1 = (f32[4,64,1024]{2,1,0:T(8,128)S(1)}, f32[4,64,1024]{2,1,0:T(8,128)}, u32[]{:S(2)}) copy-start(f32[4,64,1024]{2,1,0:T(8,128)} %param.4) | copy-start | bytes 3145732
Sparse Core Ops, SparseCore 0:
  89.0 44.7 all-gather.2
  136.3 34.5 all-gather.4
  184.0 45.3 all-reduce.6
  309.1 43.0 all-reduce.8
